TPU v7x, 256 devices: a whole 4x4x8 slice. The times are simulated.
256 devices in a mesh: batch: 64 (over y, z, core), feat: 4 (over x).
Axes of the slice: x: 4, y: 4, z: 8, core: 2. Of those that a mesh axis runs over, the one named last changes fastest.
Arguments:
- tables: bfloat16 [4, 128, 2048, 192], P('feat', 'batch'), may hold values from -3 to 3
- bag_ids: int32 [4, 128, 4, 8192], P('feat', 'batch'), may hold values from 0 to 2047
- bag_lengths: int32 [4, 128, 8192], P('feat', 'batch'), may hold values from 1 to 4
- pair_groups: int32 [16, 2], replicated, may hold values from 0 to 15
- compress: bfloat16 [16, 32, 8], P('feat'), may hold values from -1 to 1
- w_hidden: bfloat16 [16, 32, 8, 4096], P('feat'), may hold values from -0.09375 to 0.09375
- hidden_bias: float32 [4096], replicated, may hold values from -4 to 4
- norm_gain: float32 [4096], P('feat'), may hold values from 0.1 to 1.9
Outputs:
- interacted: bfloat16 [8192, 4096], P('batch', 'feat')
Inputs may be any that keep to these rules, and one draw needn't show every extreme that they name: `bag_lengths`: ids at slots from a bag's length on are ignored.
All inputs are finite; a program needn't handle non-finite values.
Results may differ from a plain program's by a relative error of at most 0.0052.
Values may be sent and summed in bfloat16 or wider, within the bound.
A program may use at most 128 MiB of HBM per device.

v0:
```python
import jax
import jax.numpy as jnp
from jax import lax
from jax.sharding import PartitionSpec as P


def take_rows(table_one, ids_one):
    return jnp.take(table_one, ids_one, axis=0)


def select_groups(source, pair_list, group_size):
    offsets = jnp.arange(group_size, dtype=jnp.int32)
    wanted = pair_list[:, :, None] * group_size + offsets[None, None, :]
    shape_out = (pair_list.shape[0], 2, group_size, source.shape[1], source.shape[2])
    return jnp.take(source, wanted.reshape(-1), axis=0).reshape(shape_out)


def squeeze_pairs(chosen, weights):
    row_blocks = chosen[:, 0]
    col_blocks = chosen[:, 1]
    gram_scale = float(chosen.shape[4]) ** (-0.5)
    gram_blocks = (
        jnp.einsum("qfbd,qgbd->qbfg", row_blocks, col_blocks, preferred_element_type=jnp.float32)
        * gram_scale
    )
    squeezed = jnp.einsum(
        "qbfg,qgk->bqfk", gram_blocks, weights.astype(jnp.float32), precision=lax.Precision.HIGHEST
    )
    return squeezed.astype(jnp.bfloat16)


def body(tables, bag_ids, bag_lengths, pair_groups, compress, w_hidden, hidden_bias, norm_gain):
    own_tables = tables[0]
    own_ids = bag_ids[0]
    own_lengths = bag_lengths[0]
    slot_count = own_ids.shape[1]
    pooled_sum = jnp.zeros((own_ids.shape[0], own_ids.shape[2], own_tables.shape[2]), jnp.float32)
    for slot in range(slot_count):
        looked = jax.vmap(take_rows)(own_tables, own_ids[:, slot, :])
        live = (own_lengths > slot)[:, :, None]
        pooled_sum = pooled_sum + jnp.where(live, looked.astype(jnp.float32), 0.0)
    pooled = pooled_sum.astype(jnp.bfloat16)
    feature_tile = lax.all_to_all(pooled, "batch", split_axis=1, concat_axis=0, tiled=True)
    samples = feature_tile.shape[1]
    pair_count = compress.shape[0]
    group_size = compress.shape[1]
    first_pair = lax.axis_index("feat") * pair_count
    local_pairs = lax.dynamic_slice_in_dim(pair_groups, first_pair, pair_count, 0)
    everything = lax.all_gather(feature_tile, "feat", axis=0, tiled=True)
    squeezed = squeeze_pairs(select_groups(everything, local_pairs, group_size), compress)
    squeezed = squeezed.reshape(samples, -1)
    w_flat = w_hidden.reshape(-1, w_hidden.shape[3])
    hid_local = norm_gain.shape[0]
    hid_total = hid_local * lax.axis_size("feat")
    own_start = lax.axis_index("feat") * hid_local
    hidden = lax.psum_scatter(
        lax.dot_general(
            w_flat, squeezed, (((0,), (1,)), ((), ())), preferred_element_type=jnp.float32
        ),
        "feat",
        scatter_dimension=0,
        tiled=True,
    )
    local_bias = lax.dynamic_slice_in_dim(hidden_bias, own_start, hid_local, 0)
    hidden = hidden + local_bias[:, None]
    row_sum, row_squares = lax.psum(
        (jnp.sum(hidden, axis=0), jnp.sum(hidden * hidden, axis=0)), "feat"
    )
    row_mean = row_sum / hid_total
    spread = row_squares / hid_total - row_mean * row_mean
    normed = (hidden - row_mean[None, :]) * lax.rsqrt(spread + 1e-05)[None, :] * norm_gain[:, None]
    return jax.nn.silu(normed).T.astype(jnp.bfloat16)


def solution(mesh):
    in_specs = (
        P("feat", "batch", None, None),
        P("feat", "batch", None, None),
        P("feat", "batch", None),
        P(),
        P("feat", None, None),
        P("feat", None, None, None),
        P(),
        P("feat"),
    )
    out_specs = P("batch", "feat")
    return jax.shard_map(body, mesh=mesh, in_specs=in_specs, out_specs=out_specs, check_vma=False)
```

profile of v0, /device:TPU:8, one launch (start us, length us, event | category | flops | bytes accessed | tf_op | source)
XLA Modules:
  0.0 1334.6 jit_solution(744671372483452733)
XLA Ops:
  6.5 0.0 copy-start
  6.5 0.0 all-gather.2.cloned.1.call-start
  6.5 1.8 fusion.15
  8.3 0.2 fusion.12
  8.5 0.2 compare_and_fusion.2
  8.7 0.2 fusion.10
  8.9 0.2 compare_and_fusion
  9.1 2.7 copy.38
  11.9 161.2 %gather_fusion.3 = bf16[16384,192]{1,0:T(8,128)(2,1)} fusion(bf16[2,2048,192]{2,1,0:T(8,128)(2,1)S(1)} %bitcast.104, s32[16384]{0:T(1024)S(1)} %bitcast.108), kind=kCustom, calls=%fused_computation.2.clone | custom fusion | bytes 12713984 | tf_op jit(solution)/shard_map/vmap(jit(_take))/gather | solution.py:8
  173.1 161.2 %gather_fusion.4 = bf16[16384,192]{1,0:T(8,128)(2,1)} fusion(bf16[2,2048,192]{2,1,0:T(8,128)(2,1)S(1)} %bitcast.105, s32[16384]{0:T(1024)S(1)} %bitcast.109), kind=kCustom, calls=%fused_computation.3.clone | custom fusion | bytes 12713984 | tf_op jit(solution)/shard_map/vmap(jit(_take))/gather | solution.py:8
  334.3 161.1 %gather_fusion.1 = bf16[16384,192]{1,0:T(8,128)(2,1)} fusion(bf16[2,2048,192]{2,1,0:T(8,128)(2,1)S(1)} %bitcast.106, s32[16384]{0:T(1024)S(1)} %bitcast.111), kind=kCustom, calls=%fused_computation.clone | custom fusion | bytes 12713984 | tf_op jit(solution)/shard_map/vmap(jit(_take))/gather | solution.py:8
  495.4 0.0 copy-start.1
  495.4 161.2 %gather_fusion.2 = bf16[16384,192]{1,0:T(8,128)(2,1)} fusion(bf16[2,2048,192]{2,1,0:T(8,128)(2,1)S(1)} %bitcast.107, s32[16384]{0:T(1024)S(1)} %bitcast.110), kind=kCustom, calls=%fused_computation.1.clone | custom fusion | bytes 12713984 | tf_op jit(solution)/shard_map/vmap(jit(_take))/gather | solution.py:8
  656.6 1.7 copy.37
  658.3 1.7 copy.41
  660.1 1.7 copy.44
  661.8 2.2 copy.47
  664.0 0.0 copy-done.1
  664.0 0.1 compare_bitcast_fusion.3
  664.2 2.2 copy.36
  666.3 2.1 copy.40
  668.5 2.1 copy.43
  670.6 2.2 copy.46
  672.8 79.1 %add_convert_fusion = bf16[2,8192,192]{2,0,1:T(2,128)(2,1)S(1)} fusion(pred[2,8192]{0,1:T(8,128)(4,1)} %copy.46, pred[2,8192]{0,1:T(8,128)(4,1)} %copy.43, pred[2,8192]{0,1:T(8,128)(4,1)} %copy.40, pred[2,8192]{0,1:T(8,128)(4,1)} %copy.36, pred[2,8192]{0,1:T(8,128)(4,1)S(1)} %copy.37, pred[2,8192]{0,1:T(8,128)(4,1)S(1)} %copy.41, ...), kind=kLoop, calls=%fused_computation.5 | loop fusion | flops 50331648 | bytes 31588352 | tf_op jit(solution)/shard_map/convert_element_type | solution.py:42
  751.8 196.1 %all_to_all.18 = bf16[2,8192,192]{2,0,1:T(2,128)(2,1)} all-to-all(bf16[2,8192,192]{2,0,1:T(2,128)(2,1)S(1)} %add_convert_fusion), channel_id=1, replica_groups=mesh['batch'=64,'feat'=4] {'batch'}, dimensions={1} | all-to-all | bytes 12582912 | tf_op jit(solution)/shard_map/all_to_all | solution.py:43
  948.0 0.0 copy-start.3
  948.0 20.4 %copy.56 = bf16[2,64,128,192]{2,3,0,1:T(8,128)(2,1)} copy(bf16[2,64,128,192]{3,0,2,1:T(2,128)(2,1)} %bitcast.113) | data formatting | bytes 12582912 | tf_op jit(solution)/shard_map/all_to_all | solution.py:43
  968.4 0.0 all-gather.2.cloned.1.call-update
  968.4 0.2 reduce-scatter.2.cloned.1.call-start
  968.6 0.0 copy-done.3
  968.6 0.1 dynamic-slice_multiply_fusion
  968.7 0.1 copy.34
  968.8 0.1 iota_add_fusion
  968.9 0.1 add.103
  969.0 0.1 compare_and_fusion.4
  969.1 224.3 %all-gather.2.cloned.1.call-done = bf16[512,128,192]{1,2,0:T(8,128)(2,1)} async-done(((bf16[128,128,192]{1,2,0:T(8,128)(2,1)}), bf16[512,128,192]{1,2,0:T(8,128)(2,1)}) %all-gather.2.cloned.1.call-update) | async-done | bytes 25165840 | tf_op jit(solution)/shard_map/all_gather | solution.py:49
  1193.3 18.8 %gather_fusion = bf16[256,128,192]{1,2,0:T(8,128)(2,1)} fusion(bf16[512,128,192]{1,2,0:T(8,128)(2,1)} %all-gather.2.cloned.1.call-done, s32[1024]{0:T(1024)S(1)} %pad_clamp_fusion), kind=kCustom, calls=%fused_computation.4 | custom fusion | bytes 25166848 | tf_op jit(solution)/shard_map/jit(_take)/gather | solution.py:15
  1212.1 27.1 %copy.51 = bf16[4,2,32,128,192]{4,2,3,0,1:T(8,128)(2,1)} copy(bf16[4,2,32,128,192]{3,4,2,1,0:T(8,128)(2,1)} %bitcast.112) | data formatting | bytes 25165824 | tf_op jit(solution)/shard_map/jit(_take)/gather | solution.py:15
  1239.3 14.1 %broadcast_select_fusion.4 = bf16[4,2,32,128,192]{4,2,3,0,1:T(8,128)(2,1)} fusion(bf16[4,2,32,128,192]{4,2,3,0,1:T(8,128)(2,1)} %copy.51, pred[4,2,32]{2,0,1:T(4,128)(4,1)S(1)} %copy.35), kind=kLoop, calls=%fused_computation.10 | loop fusion | flops 6291456 | bytes 25166080 | tf_op jit(solution)/shard_map/jit(_take)/select_n | solution.py:15
  1253.4 11.3 broadcast_multiply_fusion
  1264.7 0.0 copy-done
  1264.7 11.9 fusion.6
  1276.6 0.0 copy-start.2
  1276.6 6.1 convolution_bitcast_fusion
  1282.7 0.0 reduce-scatter.2.cloned.1.call-update
  1282.7 0.7 dynamic_slice.7
  1283.4 32.5 %reduce-scatter.2.cloned.1.call-done = f32[1024,128]{0,1:T(8,128)} async-done(((f32[4096,128]{0,1:T(8,128)}), f32[1024,128]{0,1:T(8,128)}) %reduce-scatter.2.cloned.1.call-update) | async-done | bytes 524304 | tf_op jit(solution)/shard_map/reduce_scatter | solution.py:56
  1315.9 1.2 add_reduce_fusion
  1317.1 8.6 all-reduce
  1325.7 0.0 copy-done.2
  1325.7 2.0 fusion.9
  (8 shorter events, 0.1 us)
Async XLA Ops:
  6.5 1258.2 %copy-start = (bf16[4,32,8]{1,2,0:T(8,128)(2,1)S(1)}, bf16[4,32,8]{1,2,0:T(8,128)(2,1)}, u32[]{:S(2)}) copy-start(bf16[4,32,8]{1,2,0:T(8,128)(2,1)} %param.14) | copy-start | bytes 6148
  6.5 1186.8 %all-gather.2.cloned.1.call-start = ((), (), s32[]{:S(2)}) async-start(), calls=%async_computation.2 | async-start | bytes 31457280 | tf_op jit(solution)/shard_map/all_gather | solution.py:49
  495.4 168.6 %copy-start.1 = (s32[1,2,8192]{2,1,0:T(2,128)S(1)}, s32[1,2,8192]{2,1,0:T(2,128)}, u32[]{:S(2)}) copy-start(s32[1,2,8192]{2,1,0:T(2,128)} %param.12) | copy-start | bytes 196612
  948.0 20.6 %copy-start.3 = (s32[16,2]{0,1:T(2,128)S(1)}, s32[16,2]{0,1:T(2,128)}, u32[]{:S(2)}) copy-start(s32[16,2]{0,1:T(2,128)} %param.13) | copy-start | bytes 388
  968.4 347.6 %reduce-scatter.2.cloned.1.call-start = ((), (), s32[]{:S(2)}) async-start(), calls=%async_computation.3 | async-start | bytes 2621440 | tf_op jit(solution)/shard_map/reduce_scatter | solution.py:56
  1276.6 49.1 %copy-start.2 = (f32[1024]{0:T(1024)S(1)}, f32[1024]{0:T(1024)}, u32[]{:S(2)}) copy-start(f32[1024]{0:T(1024)} %param.17) | copy-start | bytes 12292
Sparse Core Ops, SparseCore 0:
  968.5 224.7 all-gather.1
  1282.8 33.0 reduce-scatter.1
where the time goes:
time: 1340 us; the launch traced here: 1330 us
  local copies, waits for them, and re-layouts  732 us (55%)
  waiting for transfers between devices  257 us (19%)
  blocking collectives  205 us (15%)
  other arithmetic  97.5 us (7%)
  matrix products  29.3 us (2%)
  between operations  13.6 us (1%)
    gather x4, local copies, waits for them, and re-layouts, take_rows(): return jnp.take(table_one, ids_one, axis=0)  645 us
    all_gather x1, waiting for transfers between devices, body(): everything = lax.all_gather(feature_tile, 'feat', axis=0, tiled=True)  224 us
    all_to_all x1, blocking collectives, body(): lax.all_to_all(pooled, 'batch', split_axis=1, concat_axis=0, tiled=True)  196 us
    convert_element_type x1, other arithmetic, body(): pooled = pooled_sum.astype(jnp.bfloat16)  79.1 us
    gather x2, local copies, waits for them, and re-layouts, select_groups(): return jnp.take(source, wanted.reshape(-1), axis=0).reshape(shape_out)  45.9 us
    reduce_scatter x1, waiting for transfers between devices, body(): lax.psum_scatter(lax.dot_general(w_flat, squeezed, (((0,), (1,)), ((), ()...  32.5 us
  transfers between devices with their start and end apart: 2, of which 2 were waited for; matrix products, arithmetic and copies ran while one was open for 0% of the time, Pallas kernels for 0%

commit v1 on v0

v1 whole, which is shorter than its diff:
```python
import jax
import jax.numpy as jnp
from jax import lax
from jax.experimental import pallas as pl
from jax.experimental.pallas import tpu as pltpu
from jax.sharding import PartitionSpec as P

MESH = pl.DeviceIdType.MESH
BF = jnp.bfloat16
F32 = jnp.float32
NY, NZ, NX = 4, 8, 4
SRC = 256
SD = 32
DIM = 192
ROWS = 2048
LANES = 2 * DIM
CH = 256
NCH = 32
LAG = 8


def kernel(tt, ids, lens, pick, cpart, w_hbm, bias, gain, out,
           oh, send, recv, rf, cexp, expand, sqf, sq, lhs, w, part, partin, own, stats, statin,
           ssem, rsem, lsem, csem_s, csem_r, qsem_s, qsem_r, psem_s, psem_r, tsem_s, tsem_r, wsem):
    b = lax.axis_index("batch")
    x = lax.axis_index("feat")
    y = b // 16
    z = lax.rem(b // 2, NZ)
    c = lax.rem(b, 2)
    me = x * 64 + b

    bar = pltpu.get_barrier_semaphore()

    @pl.loop(1, 256)
    def _(i):
        tx = lax.rem(x + i // 64, NX)
        r = lax.rem(i, 64)
        ty = lax.rem(y + r // 16, NY)
        tz = lax.rem(z + lax.rem(r // 2, NZ), NZ)
        tc = lax.rem(c + lax.rem(r, 2), 2)
        pl.semaphore_signal(bar, inc=1, device_id=((ty * NZ + tz) * 2 + tc, tx), device_id_type=MESH)

    wcopy = pltpu.make_async_copy(w_hbm, w, wsem)
    wcopy.start()

    row = lax.broadcasted_iota(jnp.int32, (256, 256), 0)
    col = lax.broadcasted_iota(jnp.int32, (256, 256), 1)
    expand[...] = ((row // 128 == lax.rem(col // 8, 2)) & (lax.rem(row, 8) == lax.rem(col, 8))).astype(F32).astype(BF)

    def where_to(t):
        cy = lax.rem(y + t // 8, NY)
        cz = lax.rem(z + lax.rem(3 * lax.rem(t, 8) + 4, 8), NZ)
        return cy * NZ + cz

    def pool(t):
        chip = where_to(t)
        at = pl.multiple_of(chip * CH, CH)
        sums = []
        for e in range(2):
            length = lens[pl.ds(e, 1), pl.ds(at, CH)]
            live = [jnp.where(length > k, ids[e, pl.ds(k, 1), pl.ds(at, CH)], -4096 - k) for k in range(4)]
            keyed, counts = [], []
            for k in range(4):
                count = jnp.ones((1, CH), F32)
                for m in range(k + 1, 4):
                    count = count + jnp.where(live[m] == live[k], 1.0, 0.0)
                key = live[k]
                for m in range(k):
                    key = jnp.where(live[m] == live[k], -4096, key)
                keyed.append(key)
                counts.append(count.astype(BF))
            base = lax.broadcasted_iota(jnp.int32, (256, CH), 0).astype(F32).astype(BF)
            for j in range(8):
                hot = jnp.zeros((256, CH), BF)
                for k in range(3, -1, -1):
                    key = (keyed[k] - 256 * j).astype(F32).astype(BF)
                    hot = jnp.where(base == key, counts[k], hot)
                oh[e, pl.ds(j * 256, 256), :] = hot
            sums.append(jnp.dot(tt[e], oh[e], preferred_element_type=F32))
        full = jnp.concatenate([sums[0], sums[1][128:], sums[1][:128]], axis=0)
        send[chip] = full.T.astype(BF).reshape(2, NX, SD, LANES)

    def send_one(t, dx, dc):
        chip = where_to(t)
        tx = lax.rem(x + dx, NX)
        tc = lax.rem(c + dc, 2)
        pltpu.make_async_remote_copy(
            src_ref=send.at[chip, tc, tx], dst_ref=recv.at[me], send_sem=ssem, recv_sem=rsem,
            device_id=(chip * 2 + tc, tx), device_id_type=MESH).start()

    def send_chunk(t):
        for dx in range(NX):
            for dc in range(2):
                if dx == 0 and dc == 0:
                    @pl.when(t != 4)
                    def _():
                        send_one(t, dx, dc)
                else:
                    send_one(t, dx, dc)

    def c_copy(dx):
        tx = lax.rem(x + dx, NX)
        return pltpu.make_async_remote_copy(
            src_ref=cpart, dst_ref=cexp.at[x], send_sem=csem_s.at[dx], recv_sem=csem_r.at[dx],
            device_id=(b, tx), device_id_type=MESH)

    @pl.loop(0, NCH)
    def _(t):
        pool(t)

        @pl.when(t == LAG)
        def _():
            pl.semaphore_wait(bar, 255)
            for dx in range(1, NX):
                c_copy(dx).start()

            @pl.loop(0, LAG - 1)
            def _(u):
                send_chunk(u)

        @pl.when(t >= LAG)
        def _():
            send_chunk(t - 1)

    send_chunk(NCH - 1)
    mine = pltpu.make_async_copy(send.at[y * NZ + z, c, x], recv.at[me], lsem)
    mine.start()
    cexp[x] = cpart[...]
    for dx in range(1, NX):
        c_copy(dx).wait()
    mine.wait()
    every = pltpu.make_async_remote_copy(
        src_ref=recv.at[pl.ds(0, SRC - 1)], dst_ref=recv.at[pl.ds(0, SRC - 1)], send_sem=ssem, recv_sem=rsem,
        device_id=(b, lax.rem(x + 1, NX)), device_id_type=MESH)
    every.wait()

    @pl.loop(0, SRC // 8)
    def _(i):
        block = recv[pl.ds(i * 8, 8)].reshape(8 * SD, LANES).astype(F32)
        for q in range(3):
            rf[q, pl.ds(pl.multiple_of(i * 8 * SD, 8 * SD), 8 * SD), :] = block[:, q * 128:(q + 1) * 128]

    lane = lax.broadcasted_iota(jnp.int32, (128, 128), 1)
    pr = lax.broadcasted_iota(jnp.int32, (256, 256), 0)
    pc = lax.broadcasted_iota(jnp.int32, (256, 256), 1)
    scale = float(DIM) ** -0.5
    low = lane < 64

    @pl.loop(0, SD)
    def _(s):
        one = jnp.concatenate([rf[q, pl.ds(s, SRC, stride=SD), :] for q in range(3)], 1).astype(BF)
        u0 = jnp.dot(cexp[:, 0].reshape(128, 256), one[:, :256], preferred_element_type=F32)
        u1 = jnp.dot(cexp[:, 1].reshape(128, 256), one[:, 128:], preferred_element_type=F32)
        va = u0[:, :128] + u1[:, 128:]
        vb = jnp.where(low, u0[:, 128:], u1[:, :128])
        vb = vb + pltpu.roll(vb, 64, 1)
        vb0 = jnp.where(low, vb, 0.0)
        vb1 = jnp.where(low, 0.0, vb)

        def two(v):
            hi = v.astype(BF)
            return hi, (v - hi.astype(F32)).astype(BF)
        ah, al = two(va)
        b0h, b0l = two(vb0)
        b1h, b1l = two(vb1)
        w0 = jnp.concatenate([jnp.concatenate([ah, b0h], 1), jnp.concatenate([al, b0l], 1)], 0)
        w1 = jnp.concatenate([jnp.concatenate([b1h, ah], 1), jnp.concatenate([b1l, al], 1)], 0)
        rows = jnp.dot(pick[...], one, preferred_element_type=F32).astype(BF)
        dims = (((1,), (1,)), ((), ()))
        s0 = lax.dot_general(rows[:, :256], w0, dims, preferred_element_type=F32)
        s1 = lax.dot_general(rows[:, 128:], w1, dims, preferred_element_type=F32)
        both = jnp.concatenate([s0[:, :128] + s0[:, 128:], s1[:, :128] + s1[:, 128:]], 1) * scale
        both = jnp.where(pr // 16 == lax.rem(pc // 8, 16), both, 0.0).astype(BF)
        wide = jnp.dot(both, expand[...], preferred_element_type=F32)
        wide = jnp.where(lax.rem(pr, 16) == pc // 16, wide, 0.0)
        line = jnp.sum(wide.reshape(16, 16, 256), axis=1)
        for q in range(2):
            sqf[q, pl.ds(s, 16, stride=SD), :] = line[:, q * 128:(q + 1) * 128]

    for q in range(2):
        sq[:, :, :, q * 128:(q + 1) * 128] = sqf[q].astype(BF).reshape(4, 4, SD, 128)

    def q_copy(dx):
        tx = lax.rem(x + dx, NX)
        return pltpu.make_async_remote_copy(
            src_ref=sq.at[tx], dst_ref=lhs.at[x], send_sem=qsem_s.at[dx], recv_sem=qsem_r.at[dx],
            device_id=(b, tx), device_id_type=MESH)

    for dx in range(1, NX):
        q_copy(dx).start()
    lhs[x] = sq[x]
    wcopy.wait()
    for dx in range(1, NX):
        q_copy(dx).wait()

    def p_copy(dx):
        tx = lax.rem(x + dx, NX)
        return pltpu.make_async_remote_copy(
            src_ref=part.at[dx - 1], dst_ref=partin.at[dx - 1], send_sem=psem_s.at[dx - 1], recv_sem=psem_r.at[dx - 1],
            device_id=(b, tx), device_id_type=MESH)

    for dx in (2, 1, 3, 0):
        tx = lax.rem(x + dx, NX)

        @pl.loop(0, 4)
        def _(n):
            cols = pl.ds(pl.multiple_of(tx * 1024 + n * 256, 256), 256)
            acc = jnp.zeros((128, 256), F32)
            for p in range(4):
                acc = acc + jnp.dot(lhs[:, p].reshape(128, 256), w[p, :, cols], preferred_element_type=F32)
            here = pl.ds(pl.multiple_of(n * 256, 256), 256)
            if dx == 0:
                own[:, here] = acc + bias[:, cols]
            else:
                part[dx - 1, :, here] = acc.astype(BF)
        if dx != 0:
            p_copy(dx).start()
    for dx in range(1, NX):
        p_copy(dx).wait()
    hidden = own[...]
    for dx in range(1, NX):
        hidden = hidden + partin[dx - 1].astype(F32)
    own[...] = hidden
    rsum = jnp.sum(hidden, axis=1, keepdims=True)
    rsq = jnp.sum(hidden * hidden, axis=1, keepdims=True)
    both = jnp.where(lane == 0, rsum, jnp.where(lane == 1, rsq, 0.0))
    stats[...] = both.T[:8]

    def t_copy(dx):
        tx = lax.rem(x + dx, NX)
        return pltpu.make_async_remote_copy(
            src_ref=stats, dst_ref=statin.at[dx - 1], send_sem=tsem_s.at[dx - 1], recv_sem=tsem_r.at[dx - 1],
            device_id=(b, tx), device_id_type=MESH)

    for dx in range(1, NX):
        t_copy(dx).start()
    for dx in range(1, NX):
        t_copy(dx).wait()
    total = (stats[...] + statin[0] + statin[1] + statin[2]) * (1.0 / 4096.0)
    mean = total[0:1]
    inv = lax.rsqrt(total[1:2] - mean * mean + 1e-05)
    back = jnp.concatenate([mean, inv, jnp.zeros((126, 128), F32)], 0).T
    v = (own[...] - back[:, 0:1]) * back[:, 1:2] * gain[...]
    out[...] = (v / (1.0 + jnp.exp(-v))).astype(BF)


def body(tables, bag_ids, bag_lengths, pair_groups, compress, w_hidden, hidden_bias, norm_gain):
    x = lax.axis_index("feat")
    local = lax.dynamic_slice_in_dim(pair_groups, x * 4, 4, 0)
    comp = compress.reshape(4, 16, 2, 8).transpose(2, 0, 3, 1)
    hit = (jnp.arange(16, dtype=jnp.int32)[None, :] == local[:, 1:2])[None, :, None, :, None]
    cpart = jnp.where(hit, comp[:, :, :, None, :], jnp.zeros((), BF)).reshape(2, 32, 256)
    slots = jnp.arange(256, dtype=jnp.int32)
    want = jnp.repeat(pair_groups[:, 0], 16) * 16 + slots % 16
    pick = (want[:, None] == slots[None, :]).astype(BF)
    vm = pl.BlockSpec(memory_space=pltpu.VMEM)
    sem = pltpu.SemaphoreType.DMA
    return pl.pallas_call(
        kernel,
        out_shape=jax.ShapeDtypeStruct((128, 1024), BF),
        in_specs=[vm, vm, vm, vm, vm, pl.BlockSpec(memory_space=pl.ANY), vm, vm],
        out_specs=vm,
        scratch_shapes=[
            pltpu.VMEM((2, ROWS, CH), BF),
            pltpu.VMEM((NCH, 2, NX, SD, LANES), BF),
            pltpu.VMEM((SRC, SD, LANES), BF),
            pltpu.VMEM((3, SRC * SD, 128), F32),
            pltpu.VMEM((4, 2, 32, 256), BF),
            pltpu.VMEM((256, 256), BF),
            pltpu.VMEM((2, 16 * SD, 128), F32),
            pltpu.VMEM((4, 4, SD, 256), BF),
            pltpu.VMEM((4, 4, SD, 256), BF),
            pltpu.VMEM((4, 256, 4096), BF),
            pltpu.VMEM((3, 128, 1024), BF),
            pltpu.VMEM((3, 128, 1024), BF),
            pltpu.VMEM((128, 1024), F32),
            pltpu.VMEM((8, 128), F32),
            pltpu.VMEM((3, 8, 128), F32),
            sem, sem, sem, sem((4,)), sem((4,)), sem((4,)), sem((4,)), sem((3,)), sem((3,)), sem((3,)), sem((3,)), sem,
        ],
        compiler_params=pltpu.CompilerParams(
            collective_id=0, has_side_effects=True, vmem_limit_bytes=60 << 20),
    )(tables[0].swapaxes(1, 2), bag_ids[0], bag_lengths[0], pick, cpart,
      w_hidden.reshape(4, 256, 4096), hidden_bias.reshape(1, 4096), norm_gain.reshape(1, 1024))


def solution(mesh):
    in_specs = (
        P("feat", "batch", None, None),
        P("feat", "batch", None, None),
        P("feat", "batch", None),
        P(),
        P("feat", None, None),
        P("feat", None, None, None),
        P(),
        P("feat"),
    )
    out_specs = P("batch", "feat")
    return jax.shard_map(body, mesh=mesh, in_specs=in_specs, out_specs=out_specs, check_vma=False)
```

time: 1340 us -> 234 us (0.17)
  local copies, waits for them, and re-layouts: 732 us -> 4 us
  waiting for transfers between devices: 257 us -> 0 us
  Pallas kernels: 0 us -> 224 us
  blocking collectives: 205 us -> 0 us
  other arithmetic: 97.5 us -> 2.13 us
  matrix products: 29.3 us -> 0 us
  between operations: 13.6 us -> 0.03 us
    gather x6 -> x0, local copies, waits for them, and re-layouts: 691 us -> none  [the longest x4 645 us: take_rows(): return jnp.take(table_one, ids_one, axis=0)]
    all_gather x1 -> x0, waiting for transfers between devices: 224 us -> none  [body(): everything = lax.all_gather(feature_tile, 'feat', axis=0, tiled=True)]
    pallas_call x0 -> x1, Pallas kernels: none -> 224 us  [body(): pl.pallas_call(kernel, out_shape=jax.ShapeDtypeStruct((128, 1024), BF), i...]
    all_to_all x1 -> x0, blocking collectives: 196 us -> none  [body(): lax.all_to_all(pooled, 'batch', split_axis=1, concat_axis=0, tiled=True)]
    convert_element_type x2 -> x1, other arithmetic: 81.1 us -> 0.76 us  [body(): pick = (want[:, None] == slots[None, :]).astype(BF)]
    reduce_scatter x1 -> x0, waiting for transfers between devices: 32.5 us -> none  [body(): lax.psum_scatter(lax.dot_general(w_flat, squeezed, (((0,), (1,)), ((), ()...]
    dot_general x3 -> x0, matrix products: 29.3 us -> none  [the longest x1 11.9 us: squeeze_pairs(): jnp.einsum('qbfg,qgk->bqfk', gram_blocks, weights.astype(jnp.float32), pr...]
    all_to_all x1 -> x0, local copies, waits for them, and re-layouts: 20.4 us -> none  [body(): lax.all_to_all(pooled, 'batch', split_axis=1, concat_axis=0, tiled=True)]
  transfers between devices with their start and end apart: 2 -> 0, of which waited for: 2 -> 0; matrix products, arithmetic and copies ran while one was open for 0% -> 0% of each run, Pallas kernels for 0% -> 0%
where the time goes in v1:
time: 234 us; the launch traced here: 230 us
  Pallas kernels  224 us (96%)
  local copies, waits for them, and re-layouts  4 us (2%)
    pallas_call x1, Pallas kernels, body(): pl.pallas_call(kernel, out_shape=jax.ShapeDtypeStruct((128, 1024), BF), i...  224 us

profile of v1, /device:TPU:8, one launch (start us, length us, event | category | flops | bytes accessed | tf_op | source)
XLA Modules:
  0.0 229.7 jit_solution(14163593456033621210)
XLA Ops:
  0.0 0.7 constant_dynamic-slice_fusion
  0.8 0.1 iota_compare_fusion.1
  0.8 0.7 multiply_bitcast_fusion
  1.5 0.1 broadcast_in_dim.34
  1.6 0.1 mul.25
  1.7 0.8 copy.10
  2.5 0.1 copy.11
  2.6 0.1 broadcast_in_dim.35
  2.7 0.2 broadcast_in_dim.36
  2.8 0.8 fusion.pick
  3.6 0.2 broadcast_in_dim.39
  3.9 0.6 broadcast_select_fusion.cpart
  4.5 223.6 %shard_map.82 = bf16[128,1024]{1,0:T(8,128)(2,1)} custom-call(bf16[2,192,2048]{2,1,0:T(8,128)(2,1)} %bitcast.20, s32[2,4,8192]{2,1,0:T(4,128)} %bitcast.21, s32[2,8192]{1,0:T(2,128)} %bitcast.23, bf16[256,256]{1,0:T(8,128)(2,1)} %fusion.pick, bf16[2,32,256]{2,1,0:T(8,128)(2,1)} %broadcast_select_fusion.cpart, bf16[4,256,4096]{2,1,0:T(8,128)(2,1)} %bitcast.19, ...), custom_call_target="tpu_custom_call" | custom-call | tf_op jit(solution)/shard_map/pallas_call | solution.py:258
  228.0 1.7 copy.13
  (3 shorter events, 0.1 us)

commit v2 on v1

v2 whole, which is shorter than its diff:
```python
import jax
import jax.numpy as jnp
from jax import lax
from jax.experimental import pallas as pl
from jax.experimental.pallas import tpu as pltpu
from jax.sharding import PartitionSpec as P

MESH = pl.DeviceIdType.MESH
BF = jnp.bfloat16
F32 = jnp.float32
NY, NZ, NX = 4, 8, 4
SRC = 256
SD = 32
DIM = 192
ROWS = 2048
LANES = 2 * DIM
CH = 256
NR = 4
SPR = SD // NR
WID = 4 * SPR
UNITS = 32
UPR = UNITS // NR
LAG = 3


def kernel(tt, ids, lens, cpart, gmask, w_hbm, bias, gain, out,
           oh, send, recv, rf, cexp, perm, cs, cf, sq, lhs, w, part, partin, own, stats, statin,
           ssem, rsem, lsem, csem_s, csem_r, qsem_s, qsem_r, psem_s, psem_r, tsem_s, tsem_r, wsem):
    b = lax.axis_index("batch")
    x = lax.axis_index("feat")
    y = b // 16
    z = lax.rem(b // 2, NZ)
    c = lax.rem(b, 2)
    me = x * 64 + b

    bar = pltpu.get_barrier_semaphore()

    @pl.loop(0, 128)
    def _(i):
        tx = lax.rem(x + i // 32, NX)
        ty = lax.rem(y + lax.rem(i // 8, NY), NY)
        tz = lax.rem(z + lax.rem(i, NZ), NZ)
        at = (ty * NZ + tz) * 2
        pl.semaphore_signal(bar, inc=1, device_id=(at + 1 - c, tx), device_id_type=MESH)

        @pl.when(i != 0)
        def _():
            pl.semaphore_signal(bar, inc=1, device_id=(at + c, tx), device_id_type=MESH)

    @pl.loop(0, 16)
    def _(j):
        for p in range(4):
            pltpu.make_async_copy(
                w_hbm.at[p, pl.ds(pl.multiple_of(j * 16, 16), 16)],
                w.at[j // 4, pl.ds(pl.multiple_of(lax.rem(j, 4) * 64 + p * 16, 16), 16)], wsem).start()

    row = lax.broadcasted_iota(jnp.int32, (256, 256), 0)
    col = lax.broadcasted_iota(jnp.int32, (256, 256), 1)
    perm[...] = (col == lax.rem(row // 8, 16) * 16 + row // 128 * 8 + lax.rem(row, 8)).astype(F32).astype(BF)
    quarter = lax.broadcasted_iota(jnp.int32, (1, 128), 1) // WID

    def where_to(u, q):
        t = u * NR + q
        cy = lax.rem(y + t // 8, NY)
        cz = lax.rem(z + lax.rem(3 * lax.rem(t, 8) + 4, 8), NZ)
        return cy * NZ + cz

    def pool(r, u):
        chips = [where_to(u, q) for q in range(NR)]

        def lanes_of(ref):
            tiles = []
            for h in range(2):
                made = None
                for m in range(NR):
                    k = h * NR + m
                    at = pl.multiple_of((chips[k // 2] * 2 + k % 2) * 128, 128)
                    piece = pltpu.roll(ref[:, pl.ds(at, 128)], lax.rem(m * WID - r * WID + 128, 128), 1)
                    made = piece if m == 0 else jnp.where(quarter == m, piece, made)
                tiles.append(made)
            return jnp.concatenate(tiles, axis=1)

        both_lengths = lanes_of(lens)
        sums = []
        for e in range(2):
            length = both_lengths[e:e + 1]
            four = lanes_of(ids.at[e])
            live = [jnp.where(length > k, four[k:k + 1], -4096 - k) for k in range(4)]
            keyed, counts = [], []
            for k in range(4):
                count = jnp.ones((1, CH), F32)
                for m in range(k + 1, 4):
                    count = count + jnp.where(live[m] == live[k], 1.0, 0.0)
                key = live[k]
                for m in range(k):
                    key = jnp.where(live[m] == live[k], -4096, key)
                keyed.append(key)
                counts.append(count.astype(BF))
            base = lax.broadcasted_iota(jnp.int32, (256, CH), 0).astype(F32).astype(BF)
            for j in range(8):
                hot = jnp.zeros((256, CH), BF)
                for k in range(3, -1, -1):
                    key = (keyed[k] - 256 * j).astype(F32).astype(BF)
                    hot = jnp.where(base == key, counts[k], hot)
                oh[e, pl.ds(j * 256, 256), :] = hot
            sums.append(jnp.dot(tt[e], oh[e], preferred_element_type=F32))
        full = jnp.concatenate([sums[0], sums[1][128:], sums[1][:128]], axis=0)
        made = full.T.reshape(NR, 2, NX, SPR, LANES).astype(BF)
        for q in range(NR):
            send[r, chips[q]] = made[q]

    def send_one(r, u, q, dx, dc):
        chip = where_to(u, q)
        tx = lax.rem(x + dx, NX)
        tc = lax.rem(c + dc, 2)
        pltpu.make_async_remote_copy(
            src_ref=send.at[r, chip, tc, tx], dst_ref=recv.at[r, me], send_sem=ssem, recv_sem=rsem.at[r],
            device_id=(chip * 2 + tc, tx), device_id_type=MESH).start()

    def send_unit(t):
        r = t // UPR
        u = lax.rem(t, UPR)
        for dx in range(NX):
            for dc in range(2):
                for q in range(NR):
                    if dx == 0 and dc == 0 and q == 4 % NR:
                        @pl.when(u != 4 // NR)
                        def _():
                            send_one(r, u, q, dx, dc)
                    else:
                        send_one(r, u, q, dx, dc)

    def c_copy(dx):
        tx = lax.rem(x + dx, NX)
        return pltpu.make_async_remote_copy(
            src_ref=cpart, dst_ref=cexp.at[x], send_sem=csem_s.at[dx], recv_sem=csem_r.at[dx],
            device_id=(b, tx), device_id_type=MESH)

    @pl.loop(0, UNITS)
    def _(t):
        pool(t // UPR, lax.rem(t, UPR))

        @pl.when(t == LAG)
        def _():
            pl.semaphore_wait(bar, 255)
            for dx in range(1, NX):
                c_copy(dx).start()

            @pl.loop(0, LAG - 1)
            def _(u):
                send_unit(u)

        @pl.when(t >= LAG)
        def _():
            send_unit(t - 1)

    send_unit(UNITS - 1)

    def mine(r):
        return pltpu.make_async_copy(send.at[r, y * NZ + z, c, x], recv.at[r, me], lsem.at[r])

    for r in range(NR):
        mine(r).start()
    cexp[x] = cpart[...]
    for dx in range(1, NX):
        c_copy(dx).wait()
    pltpu.make_async_copy(w_hbm, w, wsem).wait()

    lane = lax.broadcasted_iota(jnp.int32, (128, 128), 1)
    scale = float(DIM) ** -0.5
    low = lane < 64

    def gram(s):
        one = jnp.concatenate([rf[q, pl.ds(s, SRC, stride=SPR), :] for q in range(3)], 1).astype(BF)
        u0 = jnp.dot(cexp[:, 0].reshape(128, 256), one[:, :256], preferred_element_type=F32)
        u1 = jnp.dot(cexp[:, 1].reshape(128, 256), one[:, 128:], preferred_element_type=F32)
        va = u0[:, :128] + u1[:, 128:]
        vb = jnp.where(low, u0[:, 128:], u1[:, :128])
        vb = vb + pltpu.roll(vb, 64, 1)
        vb0 = jnp.where(low, vb, 0.0)
        vb1 = jnp.where(low, 0.0, vb)

        def two(v):
            hi = v.astype(BF)
            return hi, (v - hi.astype(F32)).astype(BF)
        ah, al = two(va)
        b0h, b0l = two(vb0)
        b1h, b1l = two(vb1)
        w0 = jnp.concatenate([jnp.concatenate([ah, b0h], 1), jnp.concatenate([al, b0l], 1)], 0)
        w1 = jnp.concatenate([jnp.concatenate([b1h, ah], 1), jnp.concatenate([b1l, al], 1)], 0)
        dims = (((1,), (1,)), ((), ()))
        lines = []
        for e, (rows, ww) in enumerate(((one[:, :256], w0), (one[:, 128:], w1))):
            se = lax.dot_general(rows, ww, dims, preferred_element_type=F32)
            se = (se[:, :128] + se[:, 128:]).reshape(16, 16, 128)
            got = jnp.where(gmask[0:1, :] > 0.5, se[0], 0.0)
            for g in range(1, 16):
                got = jnp.where(gmask[g:g + 1, :] > 0.5, se[g], got)
            lines.append(got * scale)
        return jnp.concatenate(lines, 1).astype(BF)

    def q_copy(r, dx):
        tx = lax.rem(x + dx, NX)
        return pltpu.make_async_remote_copy(
            src_ref=sq.at[r, tx], dst_ref=lhs.at[r, x], send_sem=qsem_s.at[r, dx], recv_sem=qsem_r.at[r, dx],
            device_id=(b, tx), device_id_type=MESH)

    def p_copy(r, dx):
        tx = lax.rem(x + dx, NX)
        return pltpu.make_async_remote_copy(
            src_ref=part.at[r, dx - 1], dst_ref=partin.at[r, dx - 1],
            send_sem=psem_s.at[r, dx - 1], recv_sem=psem_r.at[r, dx - 1],
            device_id=(b, tx), device_id_type=MESH)

    def t_copy(r, dx):
        tx = lax.rem(x + dx, NX)
        return pltpu.make_async_remote_copy(
            src_ref=stats.at[r], dst_ref=statin.at[r, dx - 1],
            send_sem=tsem_s.at[r, dx - 1], recv_sem=tsem_r.at[r, dx - 1],
            device_id=(b, tx), device_id_type=MESH)

    @pl.loop(0, NR)
    def _(r):
        mine(r).wait()
        pltpu.make_async_remote_copy(
            src_ref=recv.at[r, pl.ds(0, SRC - 1)], dst_ref=recv.at[r, pl.ds(0, SRC - 1)],
            send_sem=ssem, recv_sem=rsem.at[r],
            device_id=(b, lax.rem(x + 1, NX)), device_id_type=MESH).wait_recv()

        @pl.loop(0, SRC // 16)
        def _(i):
            block = recv[r, pl.ds(i * 16, 16)].astype(F32).reshape(16 * SPR, LANES)
            for q in range(3):
                rf[q, pl.ds(pl.multiple_of(i * 16 * SPR, 16 * SPR), 16 * SPR), :] = block[:, q * 128:(q + 1) * 128]

        @pl.loop(0, SPR // 2)
        def _(h):
            first = gram(2 * h)
            second = gram(2 * h + 1)
            cs[pl.ds(pl.multiple_of(h * 32, 32), 32), :] = jnp.concatenate([first, second], 0)

        turned = jnp.dot(cs[...], perm[...], preferred_element_type=F32)
        cf[0] = turned[:, :128]
        cf[1] = turned[:, 128:]
        for h in range(2):
            by_row = [cf[h, pl.ds(j, SPR, stride=16), :] for j in range(16)]
            for half in range(2):
                cut = [v[:, half * 64:half * 64 + 64] for v in by_row]
                for jj in range(4):
                    sq[r, h * 2 + half, jj] = jnp.concatenate(cut[4 * jj:4 * jj + 4], 1).astype(BF)

        for dx in range(1, NX):
            q_copy(r, dx).start()
        lhs[r, x] = sq[r, x]
        for dx in range(1, NX):
            q_copy(r, dx).wait()

        for dx in (2, 1, 3, 0):
            tx = lax.rem(x + dx, NX)

            @pl.loop(0, 4)
            def _(n):
                cols = pl.ds(pl.multiple_of(tx * 1024 + n * 256, 256), 256)
                acc = jnp.zeros((WID, 256), F32)
                for jj in range(4):
                    acc = acc + jnp.dot(lhs[r, :, jj].reshape(WID, 256), w[jj, :, cols], preferred_element_type=F32)
                here = pl.ds(pl.multiple_of(n * 256, 256), 256)
                if dx == 0:
                    own[:, here] = acc + bias[:, cols]
                else:
                    part[r, dx - 1, :, here] = acc.astype(BF)
            if dx != 0:
                p_copy(r, dx).start()
        for dx in range(1, NX):
            p_copy(r, dx).wait()
        hidden = own[...]
        for dx in range(1, NX):
            hidden = hidden + partin[r, dx - 1].astype(F32)
        own[...] = hidden
        rsum = jnp.sum(hidden, axis=1, keepdims=True)
        rsq = jnp.sum(hidden * hidden, axis=1, keepdims=True)
        at = lane[:WID]
        both = jnp.where(at == 0, rsum, jnp.where(at == 1, rsq, 0.0))
        stats[r] = jnp.concatenate([both, jnp.zeros((128 - WID, 128), F32)], 0).T[:8]
        for dx in range(1, NX):
            t_copy(r, dx).start()
        for dx in range(1, NX):
            t_copy(r, dx).wait()
        total = (stats[r] + statin[r, 0] + statin[r, 1] + statin[r, 2]) * (1.0 / 4096.0)
        mean = total[0:1]
        inv = lax.rsqrt(total[1:2] - mean * mean + 1e-05)
        back = jnp.concatenate([mean, inv, jnp.zeros((126, 128), F32)], 0).T[:WID]
        v = (own[...] - back[:, 0:1]) * back[:, 1:2] * gain[...]
        out[pl.ds(pl.multiple_of(r * WID, WID), WID), :] = (v / (1.0 + jnp.exp(-v))).astype(BF)

    sent = recv.at[:, pl.ds(0, SRC - 1)]
    pltpu.make_async_remote_copy(
        src_ref=sent, dst_ref=sent, send_sem=ssem, recv_sem=rsem.at[0],
        device_id=(b, lax.rem(x + 1, NX)), device_id_type=MESH).wait_send()


def body(tables, bag_ids, bag_lengths, pair_groups, compress, w_hidden, hidden_bias, norm_gain):
    x = lax.axis_index("feat")
    local = lax.dynamic_slice_in_dim(pair_groups, x * 4, 4, 0)
    comp = compress.reshape(4, 16, 2, 8).transpose(2, 0, 3, 1)
    groups = jnp.arange(16, dtype=jnp.int32)
    hit = (groups[None, :] == local[:, 1:2])[None, :, None, :, None]
    cpart = jnp.where(hit, comp[:, :, :, None, :], jnp.zeros((), BF)).reshape(2, 32, 256)
    gmask = (groups[:, None] == jnp.repeat(pair_groups[:, 0], 8)[None, :]).astype(F32)
    vm = pl.BlockSpec(memory_space=pltpu.VMEM)
    sem = pltpu.SemaphoreType.DMA
    return pl.pallas_call(
        kernel,
        out_shape=jax.ShapeDtypeStruct((128, 1024), BF),
        in_specs=[vm, vm, vm, vm, vm, pl.BlockSpec(memory_space=pl.ANY), vm, vm],
        out_specs=vm,
        scratch_shapes=[
            pltpu.VMEM((2, ROWS, CH), BF),
            pltpu.VMEM((NR, 32, 2, NX, SPR, LANES), BF),
            pltpu.VMEM((NR, SRC, SPR, LANES), BF),
            pltpu.VMEM((3, SRC * SPR, 128), F32),
            pltpu.VMEM((4, 2, 32, 256), BF),
            pltpu.VMEM((256, 256), BF),
            pltpu.VMEM((SPR * 16, 256), BF),
            pltpu.VMEM((2, SPR * 16, 128), F32),
            pltpu.VMEM((NR, 4, 4, SPR, 256), BF),
            pltpu.VMEM((NR, 4, 4, SPR, 256), BF),
            pltpu.VMEM((4, 256, 4096), BF),
            pltpu.VMEM((NR, 3, WID, 1024), BF),
            pltpu.VMEM((NR, 3, WID, 1024), BF),
            pltpu.VMEM((WID, 1024), F32),
            pltpu.VMEM((NR, 8, 128), F32),
            pltpu.VMEM((NR, 3, 8, 128), F32),
            sem, sem((NR,)), sem((NR,)), sem((4,)), sem((4,)), sem((NR, 4)), sem((NR, 4)),
            sem((NR, 3)), sem((NR, 3)), sem((NR, 3)), sem((NR, 3)), sem,
        ],
        compiler_params=pltpu.CompilerParams(
            collective_id=0, has_side_effects=True, vmem_limit_bytes=60 << 20),
    )(tables[0].swapaxes(1, 2), bag_ids[0], bag_lengths[0], cpart, gmask,
      w_hidden.reshape(4, 256, 4096), hidden_bias.reshape(1, 4096), norm_gain.reshape(1, 1024))


def solution(mesh):
    in_specs = (
        P("feat", "batch", None, None),
        P("feat", "batch", None, None),
        P("feat", "batch", None),
        P(),
        P("feat", None, None),
        P("feat", None, None, None),
        P(),
        P("feat"),
    )
    out_specs = P("batch", "feat")
    return jax.shard_map(body, mesh=mesh, in_specs=in_specs, out_specs=out_specs, check_vma=False)
```

time: 234 us -> 182 us (0.78); the launches traced: 230 us -> 182 us
  Pallas kernels: 224 us -> 176 us
    pallas_call x1, Pallas kernels: 224 us -> 176 us  [body(): pl.pallas_call(kernel, out_shape=jax.ShapeDtypeStruct((128, 1024), BF), i...]
where the time goes in v2:
time: 182 us
  Pallas kernels  176 us (97%)
  local copies, waits for them, and re-layouts  4.67 us (3%)
    pallas_call x1, Pallas kernels, body(): pl.pallas_call(kernel, out_shape=jax.ShapeDtypeStruct((128, 1024), BF), i...  176 us

profile of v2, /device:TPU:8, one launch (start us, length us, event | category | flops | bytes accessed | tf_op | source)
XLA Modules:
  0.0 181.9 jit_solution(17093777150573274353)
XLA Ops:
  0.0 0.7 slice_bitcast_fusion
  0.7 0.7 constant_dynamic-slice_fusion
  1.4 0.1 iota_compare_fusion.1
  1.5 0.1 broadcast_in_dim.39
  1.6 0.1 eq.39
  1.7 0.6 fusion.gmask
  2.3 0.8 copy.10
  3.1 0.1 copy.11
  3.2 0.1 broadcast_in_dim.33
  3.3 0.2 broadcast_in_dim.34
  3.5 0.2 broadcast_in_dim.37
  3.7 0.6 broadcast_select_fusion.cpart
  4.3 175.9 %shard_map.82 = bf16[128,1024]{1,0:T(8,128)(2,1)} custom-call(bf16[2,192,2048]{2,1,0:T(8,128)(2,1)} %bitcast.20, s32[2,4,8192]{2,1,0:T(4,128)} %bitcast.21, s32[2,8192]{1,0:T(2,128)} %bitcast.23, bf16[2,32,256]{2,1,0:T(8,128)(2,1)} %broadcast_select_fusion.cpart, f32[16,128]{1,0:T(8,128)} %fusion.gmask, bf16[4,256,4096]{2,1,0:T(8,128)(2,1)} %bitcast.19, ...), custom_call_target="tpu_custom_call" | custom-call | tf_op jit(solution)/shard_map/pallas_call | solution.py:312
  180.2 1.7 copy.13
  (2 shorter events, 0.0 us)

commit v3 on v2

--- a/solution.py
+++ b/solution.py
@@ -23,8 +23,8 @@
 LAG = 3
 
 
-def kernel(tt, ids, lens, cpart, gmask, w_hbm, bias, gain, out,
-           oh, send, recv, rf, cexp, perm, cs, cf, sq, lhs, w, part, partin, own, stats, statin,
+def kernel(tt, ids, lens, pairs, comp, w_hbm, bias, gain, out,
+           oh, send, recv, rf, cpart, gmask, cexp, perm, cs, cf, sq, lhs, w, part, partin, own, stats, statin,
            ssem, rsem, lsem, csem_s, csem_r, qsem_s, qsem_r, psem_s, psem_r, tsem_s, tsem_r, wsem):
     b = lax.axis_index("batch")
     x = lax.axis_index("feat")
@@ -35,17 +35,15 @@
 
     bar = pltpu.get_barrier_semaphore()
 
-    @pl.loop(0, 128)
-    def _(i):
-        tx = lax.rem(x + i // 32, NX)
-        ty = lax.rem(y + lax.rem(i // 8, NY), NY)
-        tz = lax.rem(z + lax.rem(i, NZ), NZ)
-        at = (ty * NZ + tz) * 2
-        pl.semaphore_signal(bar, inc=1, device_id=(at + 1 - c, tx), device_id_type=MESH)
-
-        @pl.when(i != 0)
-        def _():
-            pl.semaphore_signal(bar, inc=1, device_id=(at + c, tx), device_id_type=MESH)
+    along_z = [lax.rem(z + k, NZ) * 2 for k in range(NZ)]
+    for dx in range(NX):
+        tx = lax.rem(x + dx, NX)
+        for dy in range(NY):
+            plane = lax.rem(y + dy, NY) * (2 * NZ)
+            for k in range(NZ):
+                if dx + dy + k > 0:
+                    pl.semaphore_signal(bar, inc=1, device_id=(plane + along_z[k] + c, tx), device_id_type=MESH)
+                pl.semaphore_signal(bar, inc=1, device_id=(plane + along_z[k] + 1 - c, tx), device_id_type=MESH)
 
     @pl.loop(0, 16)
     def _(j):
@@ -57,11 +55,27 @@
     row = lax.broadcasted_iota(jnp.int32, (256, 256), 0)
     col = lax.broadcasted_iota(jnp.int32, (256, 256), 1)
     perm[...] = (col == lax.rem(row // 8, 16) * 16 + row // 128 * 8 + lax.rem(row, 8)).astype(F32).astype(BF)
+    lane_pair = lax.broadcasted_iota(jnp.int32, (16, 128), 1) // 8
+    first = jnp.zeros((16, 128), jnp.int32)
+    for p in range(16):
+        first = jnp.where(lane_pair == p, pairs[0, p], first)
+    gmask[...] = (first == lax.broadcasted_iota(jnp.int32, (16, 128), 0)).astype(F32)
+    row_pair = lax.broadcasted_iota(jnp.int32, (32, 256), 0) // 8
+    second = jnp.zeros((32, 256), jnp.int32)
+    for p in range(4):
+        second = jnp.where(row_pair == p, pairs[1, x * 4 + p], second)
+    hit = second == lax.broadcasted_iota(jnp.int32, (32, 256), 1) // 16
+    slot = lax.broadcasted_iota(jnp.int32, (32, 256), 0)
+    member = lax.rem(lax.broadcasted_iota(jnp.int32, (32, 256), 1), 16)
+    for e in range(2):
+        spread = (slot == 2 * member + e).astype(F32).astype(BF)
+        cpart[e] = jnp.where(hit, jnp.dot(comp[...], spread, preferred_element_type=F32), 0.0).astype(BF)
+
     quarter = lax.broadcasted_iota(jnp.int32, (1, 128), 1) // WID
 
     def where_to(u, q):
         t = u * NR + q
-        cy = lax.rem(y + t // 8, NY)
+        cy = lax.rem(y + q + t // 8, NY)
         cz = lax.rem(z + lax.rem(3 * lax.rem(t, 8) + 4, 8), NZ)
         return cy * NZ + cz
 
@@ -120,9 +134,10 @@
     def send_unit(t):
         r = t // UPR
         u = lax.rem(t, UPR)
-        for dx in range(NX):
+        for shift in range(NX):
             for dc in range(2):
                 for q in range(NR):
+                    dx = (shift + q) % NX
                     if dx == 0 and dc == 0 and q == 4 % NR:
                         @pl.when(u != 4 // NR)
                         def _():
@@ -300,25 +315,20 @@
 
 
 def body(tables, bag_ids, bag_lengths, pair_groups, compress, w_hidden, hidden_bias, norm_gain):
-    x = lax.axis_index("feat")
-    local = lax.dynamic_slice_in_dim(pair_groups, x * 4, 4, 0)
-    comp = compress.reshape(4, 16, 2, 8).transpose(2, 0, 3, 1)
-    groups = jnp.arange(16, dtype=jnp.int32)
-    hit = (groups[None, :] == local[:, 1:2])[None, :, None, :, None]
-    cpart = jnp.where(hit, comp[:, :, :, None, :], jnp.zeros((), BF)).reshape(2, 32, 256)
-    gmask = (groups[:, None] == jnp.repeat(pair_groups[:, 0], 8)[None, :]).astype(F32)
     vm = pl.BlockSpec(memory_space=pltpu.VMEM)
     sem = pltpu.SemaphoreType.DMA
     return pl.pallas_call(
         kernel,
         out_shape=jax.ShapeDtypeStruct((128, 1024), BF),
-        in_specs=[vm, vm, vm, vm, vm, pl.BlockSpec(memory_space=pl.ANY), vm, vm],
+        in_specs=[vm, vm, vm, pl.BlockSpec(memory_space=pltpu.SMEM), vm, pl.BlockSpec(memory_space=pl.ANY), vm, vm],
         out_specs=vm,
         scratch_shapes=[
             pltpu.VMEM((2, ROWS, CH), BF),
             pltpu.VMEM((NR, 32, 2, NX, SPR, LANES), BF),
             pltpu.VMEM((NR, SRC, SPR, LANES), BF),
             pltpu.VMEM((3, SRC * SPR, 128), F32),
+            pltpu.VMEM((2, 32, 256), BF),
+            pltpu.VMEM((16, 128), F32),
             pltpu.VMEM((4, 2, 32, 256), BF),
             pltpu.VMEM((256, 256), BF),
             pltpu.VMEM((SPR * 16, 256), BF),
@@ -336,7 +346,8 @@
         ],
         compiler_params=pltpu.CompilerParams(
             collective_id=0, has_side_effects=True, vmem_limit_bytes=60 << 20),
-    )(tables[0].swapaxes(1, 2), bag_ids[0], bag_lengths[0], cpart, gmask,
+    )(tables[0].swapaxes(1, 2), bag_ids[0], bag_lengths[0], pair_groups.T,
+      compress.swapaxes(1, 2).reshape(32, 32),
       w_hidden.reshape(4, 256, 4096), hidden_bias.reshape(1, 4096), norm_gain.reshape(1, 1024))
 
 

time: 182 us -> 175 us (0.962)
  Pallas kernels: 176 us -> 173 us
  local copies, waits for them, and re-layouts: 4.67 us -> 1.67 us
    pallas_call x1, Pallas kernels: 176 us -> 173 us  [body(): pl.pallas_call(kernel, out_shape=jax.ShapeDtypeStruct((128, 1024), BF), i...]
where the time goes in v3:
time: 175 us
  Pallas kernels  173 us (99%)
    pallas_call x1, Pallas kernels, body(): pl.pallas_call(kernel, out_shape=jax.ShapeDtypeStruct((128, 1024), BF), i...  173 us

profile of v3, /device:TPU:8, one launch (start us, length us, event | category | flops | bytes accessed | tf_op | source)
XLA Modules:
  0.0 175.1 jit_solution(3123719336823408259)
XLA Ops:
  0.0 173.4 %shard_map.82 = bf16[128,1024]{1,0:T(8,128)(2,1)} custom-call(bf16[2,192,2048]{2,1,0:T(8,128)(2,1)} %bitcast.13, s32[2,4,8192]{2,1,0:T(4,128)} %bitcast.14, s32[2,8192]{1,0:T(2,128)} %bitcast.15, s32[2,16]{1,0:T(2,128)} %bitcast.19, bf16[32,32]{1,0:T(8,128)(2,1)} %bitcast.17, bf16[4,256,4096]{2,1,0:T(8,128)(2,1)} %bitcast.12, f32[1,4096]{1,0:T(1,128)} %bitcast.16, ...), custom_call_target="tpu_custom_call" | custom-call | tf_op jit(solution)/shard_map/pallas_call | solution.py:320
  173.5 1.7 copy.10

commit v4 on v3

--- a/solution.py
+++ b/solution.py
@@ -23,9 +23,9 @@
 LAG = 3
 
 
-def kernel(tt, ids, lens, pairs, comp, w_hbm, bias, gain, out,
-           oh, send, recv, rf, cpart, gmask, cexp, perm, cs, cf, sq, lhs, w, part, partin, own, stats, statin,
-           ssem, rsem, lsem, csem_s, csem_r, qsem_s, qsem_r, psem_s, psem_r, tsem_s, tsem_r, wsem):
+def kernel(tt_hbm, ids_hbm, lens_hbm, pairs, comp, w_hbm, bias, gain, out,
+           tt, ids, lens, oh, send, recv, rf, cpart, gmask, cexp, perm, cs, cf, sq, lhs, w, part, partin, own, stats, statin,
+           ssem, rsem, lsem, csem_s, csem_r, qsem_s, qsem_r, psem_s, psem_r, tsem_s, tsem_r, wsem, isem):
     b = lax.axis_index("batch")
     x = lax.axis_index("feat")
     y = b // 16
@@ -36,14 +36,19 @@
     bar = pltpu.get_barrier_semaphore()
 
     along_z = [lax.rem(z + k, NZ) * 2 for k in range(NZ)]
-    for dx in range(NX):
-        tx = lax.rem(x + dx, NX)
-        for dy in range(NY):
+    for dx in (2, 1, 3, 0):
+        tx = lax.rem(x + dx, NX)
+        for dy in (2, 1, 3, 0):
             plane = lax.rem(y + dy, NY) * (2 * NZ)
-            for k in range(NZ):
+            for k in (4, 3, 5, 2, 6, 1, 7, 0):
                 if dx + dy + k > 0:
                     pl.semaphore_signal(bar, inc=1, device_id=(plane + along_z[k] + c, tx), device_id_type=MESH)
                 pl.semaphore_signal(bar, inc=1, device_id=(plane + along_z[k] + 1 - c, tx), device_id_type=MESH)
+
+    loads = [pltpu.make_async_copy(tt_hbm, tt, isem.at[0]), pltpu.make_async_copy(ids_hbm, ids, isem.at[1]),
+             pltpu.make_async_copy(lens_hbm, lens, isem.at[2])]
+    for load in loads:
+        load.start()
 
     @pl.loop(0, 16)
     def _(j):
@@ -72,6 +77,9 @@
         cpart[e] = jnp.where(hit, jnp.dot(comp[...], spread, preferred_element_type=F32), 0.0).astype(BF)
 
     quarter = lax.broadcasted_iota(jnp.int32, (1, 128), 1) // WID
+
+    for load in loads:
+        load.wait()
 
     def where_to(u, q):
         t = u * NR + q
@@ -316,13 +324,17 @@
 
 def body(tables, bag_ids, bag_lengths, pair_groups, compress, w_hidden, hidden_bias, norm_gain):
     vm = pl.BlockSpec(memory_space=pltpu.VMEM)
+    far = pl.BlockSpec(memory_space=pl.ANY)
     sem = pltpu.SemaphoreType.DMA
     return pl.pallas_call(
         kernel,
         out_shape=jax.ShapeDtypeStruct((128, 1024), BF),
-        in_specs=[vm, vm, vm, pl.BlockSpec(memory_space=pltpu.SMEM), vm, pl.BlockSpec(memory_space=pl.ANY), vm, vm],
+        in_specs=[far, far, far, pl.BlockSpec(memory_space=pltpu.SMEM), vm, far, vm, vm],
         out_specs=vm,
         scratch_shapes=[
+            pltpu.VMEM((2, DIM, ROWS), BF),
+            pltpu.VMEM((2, 4, 8192), jnp.int32),
+            pltpu.VMEM((2, 8192), jnp.int32),
             pltpu.VMEM((2, ROWS, CH), BF),
             pltpu.VMEM((NR, 32, 2, NX, SPR, LANES), BF),
             pltpu.VMEM((NR, SRC, SPR, LANES), BF),
@@ -342,7 +354,7 @@
             pltpu.VMEM((NR, 8, 128), F32),
             pltpu.VMEM((NR, 3, 8, 128), F32),
             sem, sem((NR,)), sem((NR,)), sem((4,)), sem((4,)), sem((NR, 4)), sem((NR, 4)),
-            sem((NR, 3)), sem((NR, 3)), sem((NR, 3)), sem((NR, 3)), sem,
+            sem((NR, 3)), sem((NR, 3)), sem((NR, 3)), sem((NR, 3)), sem, sem((3,)),
         ],
         compiler_params=pltpu.CompilerParams(
             collective_id=0, has_side_effects=True, vmem_limit_bytes=60 << 20),

time: 175 us -> 176 us (level)
  no operation moved by 1% of the time
where the time goes in v4:
time: 176 us; the launch traced here: 175 us
  Pallas kernels  174 us (99%)
    pallas_call x1, Pallas kernels, body(): pl.pallas_call(kernel, out_shape=jax.ShapeDtypeStruct((128, 1024), BF), i...  174 us

profile of v4, /device:TPU:8, one launch (start us, length us, event | category | flops | bytes accessed | tf_op | source)
XLA Modules:
  0.0 175.3 jit_solution(7607253987295558775)
XLA Ops:
  0.0 173.6 %shard_map.82 = bf16[128,1024]{1,0:T(8,128)(2,1)} custom-call(bf16[2,192,2048]{2,1,0:T(8,128)(2,1)} %bitcast.13, s32[2,4,8192]{2,1,0:T(4,128)} %bitcast.14, s32[2,8192]{1,0:T(2,128)} %bitcast.15, s32[2,16]{1,0:T(2,128)} %bitcast.19, bf16[32,32]{1,0:T(8,128)(2,1)} %bitcast.17, bf16[4,256,4096]{2,1,0:T(8,128)(2,1)} %bitcast.12, f32[1,4096]{1,0:T(1,128)} %bitcast.16, ...), custom_call_target="tpu_custom_call" | custom-call | tf_op jit(solution)/shard_map/pallas_call | solution.py:329
  173.6 1.7 copy.10
